TPU v7x, 128 devices: a whole 4x4x4 slice. The times are simulated.
128 devices in a mesh: row: 16 (over y, z), col: 8 (over x, core).
Axes of the slice: x: 4, y: 4, z: 4, core: 2. Of those that a mesh axis runs over, the one named last changes fastest.
Arguments:
- matrix: float32 [18432, 18432], P('row', 'col'), as said below
Outputs:
- updated: float32 [18432, 18432], P('row', 'col')
- reflectors: float32 [18432, 512], P('row')
Inputs may be any that keep to these rules, and one draw needn't show every extreme that they name: matrix is symmetric.
All inputs are finite; a program needn't handle non-finite values.
Results may differ from a plain program's by a relative error of at most 0.00016.
Values sent between devices are 32-bit elements; how exact they have to be, the bound alone decides.
A program may use at most 128 MiB of HBM per device.

v0:
```python
import jax
import jax.numpy as jnp
from jax import lax
from jax.sharding import PartitionSpec as P

BAND = 256
PANELS = 2
HIGH = lax.Precision.HIGHEST


def mm(a, b):
    return jnp.dot(a, b, precision=HIGH)


def mm_tn(a, b):
    return lax.dot_general(a, b, (((0,), (0,)), ((), ())), precision=HIGH)


def mm_nt(a, b):
    return lax.dot_general(a, b, (((1,), (1,)), ((), ())), precision=HIGH)


def transpose_exchange(x, rows, cols):
    both = ("row", "col")
    first = []
    second = []
    for s in range(rows):
        for j in range(cols):
            src = s * cols + j
            first.append((src, (2 * j + s % 2) * cols + s // 2))
            second.append((src, (2 * j + 1 - s % 2) * cols + s // 2))
    got1 = lax.ppermute(x, both, first)
    got2 = lax.ppermute(x, both, second)
    odd_row = lax.axis_index("row") % 2 == 1
    even = jnp.where(odd_row, got2, got1)
    odd = jnp.where(odd_row, got1, got2)
    return jnp.concatenate([even, odd], axis=0)


def small_factors(gram, top):
    identity = jnp.eye(BAND, dtype=jnp.float32)
    low = jnp.linalg.cholesky(gram)
    low_inv = jax.scipy.linalg.solve_triangular(low, identity, lower=True)
    shifted = identity + mm_nt(top, low_inv)
    second = jnp.linalg.cholesky(mm_nt(shifted, shifted))
    second_inv = jax.scipy.linalg.solve_triangular(second, identity, lower=True)
    transform = mm_tn(shifted, mm_tn(second_inv, second_inv))
    return (low_inv, transform)


def body(a):
    rows = lax.psum(1, "row")
    cols = lax.psum(1, "col")
    row_count, col_count = a.shape
    r = lax.axis_index("row")
    c = lax.axis_index("col")
    row_pos = r * row_count + jnp.arange(row_count, dtype=jnp.int32)
    col_pos = c * col_count + jnp.arange(col_count, dtype=jnp.int32)
    band_idx = jnp.arange(BAND, dtype=jnp.int32)
    width = PANELS * BAND
    col_zero = c == 0
    colb = lax.psum(jnp.where(col_zero, a[:, :width], 0.0), "col")
    strip_t = transpose_exchange(colb, rows, cols)
    lo = BAND
    p0_loc = jnp.where(row_pos[:, None] >= lo, a[:, :BAND], 0.0)
    g_loc = jnp.where(col_zero, mm_tn(p0_loc, p0_loc), 0.0)
    top_loc = jnp.where(col_zero & (r == 0), a[lo : lo + BAND, :BAND], 0.0)
    gram0, top0 = lax.psum((g_loc, top_loc), ("row", "col"))
    stored = []
    current = a
    prev = None
    for k in range(PANELS):
        lo = (k + 1) * BAND
        if k == 0:
            gram, top = (gram0, top0)
            pr = jnp.where(row_pos[:, None] >= lo, colb[:, :BAND], 0.0)
            pc = jnp.where(col_pos[:, None] >= lo, strip_t[:, :BAND], 0.0)
        else:
            y_r0, w_r0, y_c0, w_c0, y_e0, w_e0 = prev
            pr = colb[:, k * BAND : (k + 1) * BAND] - mm_nt(y_r0, w_e0) - mm_nt(w_r0, y_e0)
            pc = strip_t[:, k * BAND : (k + 1) * BAND] - mm_nt(y_c0, w_e0) - mm_nt(w_c0, y_e0)
            pr = jnp.where(row_pos[:, None] >= lo, pr, 0.0)
            pc = jnp.where(col_pos[:, None] >= lo, pc, 0.0)
            g_part = mm_tn(pc, pc)
            top_part = jnp.where(col_zero, pc[lo : lo + BAND], 0.0)
            gram, top = lax.psum((g_part, top_part), "col")
        low_inv, transform = small_factors(gram, top)
        unit_r = (row_pos[:, None] - lo == band_idx[None, :]).astype(jnp.float32)
        unit_c = (col_pos[:, None] - lo == band_idx[None, :]).astype(jnp.float32)
        y_r = mm_nt(pr, low_inv) + unit_r
        y_c = mm_nt(pc, low_inv) + unit_c
        stored.append(y_r)
        xp = mm(current, y_c)
        if k + 1 < PANELS:
            nlo = (k + 1) * BAND
            ext = mm_tn(strip_t[:, nlo : nlo + BAND], y_c)
            x_r, x_e = lax.psum((xp, ext), "col")
        else:
            x_r = lax.psum(xp, "col")
        curv = lax.psum(mm_tn(y_r, xp), ("row", "col"))
        x_c = transpose_exchange(x_r, rows, cols)
        middle = mm_nt(mm(transform, curv), transform)
        w_r = mm_nt(x_r, transform) - 0.5 * mm(y_r, middle)
        w_c = mm_nt(x_c, transform) - 0.5 * mm(y_c, middle)
        current = current - mm_nt(y_r, w_c) - mm_nt(w_r, y_c)
        if k + 1 < PANELS:
            y_e = mm_nt(top, low_inv) + jnp.eye(BAND, dtype=jnp.float32)
            w_e = mm_nt(x_e, transform) - 0.5 * mm(y_e, middle)
            prev = (y_r, w_r, y_c, w_c, y_e, w_e)
    return (current, jnp.concatenate(stored, axis=1))


def solution(mesh):
    return jax.shard_map(
        body,
        mesh=mesh,
        in_specs=(P("row", "col"),),
        out_specs=(P("row", "col"), P("row", None)),
        check_vma=False,
    )
```

profile of v0, /device:TPU:1, one launch (start us, length us, event | category | flops | bytes accessed | tf_op | source)
XLA Modules:
  0.0 1369.1 jit_solution(15635334820634010336)
XLA Ops:
  21.0 137.2 %all-reduce.14.cloned.1.call-done = f32[256,256]{0,1:T(8,128)} async-done(((f32[256,256]{0,1:T(8,128)}), f32[256,256]{0,1:T(8,128)}) %all-reduce.14.cloned.1.call-update) | async-done | bytes 262160 | tf_op jit(solution)/shard_map/psum | solution.py:68
  160.3 11.7 cholesky.214
  172.0 9.8 custom-call.17
  182.1 41.3 %all-reduce.12.cloned.1.call-done = f32[1152,512]{0,1:T(8,128)} async-done(((f32[1152,512]{0,1:T(8,128)}), f32[1152,512]{0,1:T(8,128)}) %all-reduce.12.cloned.1.call-update) | async-done | bytes 2359312 | tf_op jit(solution)/shard_map/psum | solution.py:62
  223.4 7.2 collective-permute-start.1
  231.2 11.7 cholesky.231
  245.0 4.0 while.8
  249.6 19.7 %custom-call.18 = f32[2,128,128]{1,2,0:T(8,128)S(1)} custom-call(f32[2,128,128]{2,1,0:T(8,128)S(1)} %get-tuple-element.30), custom_call_target="InvertDiagBlocksLowerTriangular" | custom-call | tf_op jit(solution)/shard_map/jit(_solve_triangular)/triangular_solve | solution.py:43
  272.9 9.8 collective-permute-done
  285.4 4.2 convolution_add_fusion.1
  289.7 21.5 %fusion.94 = f32[256,1152]{1,0:T(8,128)S(1)} fusion(f32[2304,256]{1,0:T(8,128)S(1)} %convolution_add_fusion.1, f32[1152,2304]{1,0:T(8,128)} %param.4), kind=kOutput, calls=%fused_computation.198 | convolution fusion | flops 8153726976 | bytes 14155776 | tf_op jit(solution)/shard_map/dot_general | solution.py:12
  314.2 4.5 fusion.22
  318.9 293.3 %all-reduce.20.cloned.1.call-done = (f32[256,256]{0,1:T(8,128)}, f32[256,256]{1,0:T(8,128)}) async-done(((f32[256,256]{0,1:T(8,128)}, f32[256,256]{1,0:T(8,128)}), (f32[256,256]{0,1:T(8,128)}, f32[256,256]{1,0:T(8,128)})) %all-reduce.20.cloned.1.call-update) | async-done | bytes 524304 | tf_op jit(solution)/shard_map/psum | solution.py:68
  619.9 13.2 cholesky.248
  635.2 11.3 custom-call.19
  651.5 13.2 cholesky.265
  670.4 7.2 while.9
  671.3 2.9 bitcast_dynamic-update-slice_fusion.9
  677.6 21.1 %custom-call.20 = f32[2,128,128]{1,2,0:T(8,128)} custom-call(f32[2,128,128]{2,1,0:T(8,128)} %get-tuple-element.31), custom_call_target="InvertDiagBlocksLowerTriangular" | custom-call | tf_op jit(solution)/shard_map/jit(_solve_triangular)/triangular_solve | solution.py:46
  706.4 3.4 convolution_multiply_fusion.1
  709.8 3.5 fusion.100
  713.3 4.2 collective-permute-start.3
  725.7 18.9 %collective-permute-done.3 = f32[1152,256]{0,1:T(8,128)S(1)} collective-permute-done((f32[1152,256]{0,1:T(8,128)S(1)}, f32[1152,256]{0,1:T(8,128)S(1)}, u32[]{:S(2)}, u32[]{:S(2)}) %collective-permute-start.3) | collective-permute-done | bytes 1179680 | tf_op jit(solution)/shard_map/ppermute | solution.py:32
  746.4 4.1 convolution_subtract_fusion.6
  752.8 19.4 %convolution_subtract_fusion.3 = f32[1152,2304]{1,0:T(8,128)} fusion(f32[1152,2304]{1,0:T(8,128)S(1)} %bitcast.193, f32[1152,256]{0,1:T(8,128)S(1)} %convolution_add_fusion.3, f32[2304,256]{1,0:T(8,128)S(1)} %convolution_subtract_fusion.6), kind=kOutput, calls=%fused_computation.11 | convolution fusion | flops 8156381184 | bytes 24772608 | tf_op jit(solution)/shard_map/dot_general | solution.py:20
  779.0 13.9 %convolution_subtract_fusion.2 = f32[1152,2304]{1,0:T(8,128)} fusion(f32[1152,2304]{1,0:T(8,128)} %convolution_subtract_fusion.3, f32[1152,256]{1,0:T(8,128)} %copy-done.13, f32[2304,256]{1,0:T(8,128)S(1)} %convolution_add_fusion.1), kind=kOutput, calls=%fused_computation.10 | convolution fusion | flops 8156381184 | bytes 24772608 | tf_op jit(solution)/shard_map/dot_general | solution.py:20
  794.7 116.0 %all-reduce.16.cloned.1.call-done = f32[256,256]{0,1:T(8,128)} async-done(((f32[256,256]{0,1:T(8,128)}), f32[256,256]{0,1:T(8,128)}) %all-reduce.16.cloned.1.call-update) | async-done | bytes 262160 | tf_op jit(solution)/shard_map/psum | solution.py:86
  915.0 13.2 cholesky.282
  930.3 11.3 custom-call.21
  946.6 13.2 cholesky.299
  965.5 6.8 while.10
  966.1 2.8 bitcast_dynamic-update-slice_fusion.10
  972.3 21.3 %custom-call.22 = f32[2,128,128]{1,2,0:T(8,128)} custom-call(f32[2,128,128]{2,1,0:T(8,128)} %get-tuple-element.32), custom_call_target="InvertDiagBlocksLowerTriangular" | custom-call | tf_op jit(solution)/shard_map/jit(_solve_triangular)/triangular_solve | solution.py:43
  997.9 4.4 convolution_add_fusion
  1003.7 11.2 fusion.104
  1020.8 3.0 copy.15
  1025.8 53.7 %all-reduce.22.cloned.1.call-done = (f32[256,256]{0,1:T(8,128)}, f32[1152,256]{0,1:T(8,128)}) async-done(((f32[256,256]{0,1:T(8,128)}, f32[1152,256]{0,1:T(8,128)}), (f32[256,256]{0,1:T(8,128)}, f32[1152,256]{0,1:T(8,128)})) %all-reduce.22.cloned.1.call-update) | async-done | bytes 1441808 | tf_op jit(solution)/shard_map/psum | solution.py:86
  1079.4 7.2 collective-permute-start.5
  1089.4 11.7 cholesky.316
  1101.8 9.8 custom-call.23
  1112.1 11.7 cholesky.333
  1126.0 4.2 while.11
  1130.3 19.8 %custom-call.24 = f32[2,128,128]{1,2,0:T(8,128)S(1)} custom-call(f32[2,128,128]{2,1,0:T(8,128)S(1)} %get-tuple-element.33), custom_call_target="InvertDiagBlocksLowerTriangular" | custom-call | tf_op jit(solution)/shard_map/jit(_solve_triangular)/triangular_solve | solution.py:46
  1152.3 163.1 %all-reduce.18.cloned.1.call-done = f32[256,256]{1,0:T(8,128)} async-done(((f32[256,256]{1,0:T(8,128)}), f32[256,256]{1,0:T(8,128)}) %all-reduce.18.cloned.1.call-update) | async-done | bytes 262160 | tf_op jit(solution)/shard_map/psum | solution.py:100
  1318.3 3.5 fusion.110
  1327.9 4.3 convolution_subtract_fusion.4
  1332.3 18.1 %convolution_subtract_fusion.1 = f32[1152,2304]{1,0:T(8,128)S(1)} fusion(f32[1152,2304]{1,0:T(8,128)S(1)} %bitcast.191, f32[1152,256]{0,1:T(8,128)S(1)} %copy-done.9, f32[2304,256]{1,0:T(8,128)S(1)} %convolution_subtract_fusion.4), kind=kOutput, calls=%fused_computation.9 | convolution fusion | flops 8156381184 | bytes 24772608 | tf_op jit(solution)/shard_map/dot_general | solution.py:20
  1350.3 11.5 convolution_subtract_fusion
  (255 shorter events, 136.4 us)
Async XLA Ops:
  7.2 151.0 %all-reduce.14.cloned.1.call-start = ((), (), s32[]{:S(2)}) async-start(), calls=%async_computation.1 | async-start | bytes 524288 | tf_op jit(solution)/shard_map/psum | solution.py:68
  10.8 212.5 %all-reduce.12.cloned.1.call-start = ((), (), s32[]{:S(2)}) async-start(), calls=%async_computation | async-start | bytes 4718592 | tf_op jit(solution)/shard_map/psum | solution.py:62
  16.0 596.2 %all-reduce.20.cloned.1.call-start = ((), (), s32[]{:S(2)}) async-start(), calls=%async_computation.4 | async-start | bytes 1048576 | tf_op jit(solution)/shard_map/psum | solution.py:68
  20.2 249.3 %copy-start.19 = (f32[256,256]{1,0:T(8,128)}, f32[256,256]{1,0:T(8,128)S(1)}, u32[]{:S(2)}) copy-start(f32[256,256]{1,0:T(8,128)S(1)} %fusion.39) | copy-start | bytes 786436
  223.4 49.5 %collective-permute-start.1 = (f32[1152,512]{0,1:T(8,128)}, f32[1152,512]{0,1:T(8,128)}, u32[]{:S(2)}, u32[]{:S(2)}) collective-permute-start(f32[1152,512]{0,1:T(8,128)} %all-reduce.12.cloned.1.call-done), channel_id=1, source_target_pairs={{0,0},{1,16},{2,32},{3,48},{4,64},{5,80},{6,96},{7,112},{8,8},{9,2... | collective-permute-start | bytes 7077896 | tf_op jit(solution)/shard_map/ppermute | solution.py:32
  230.6 52.1 %collective-permute-start = (f32[1152,512]{0,1:T(8,128)}, f32[1152,512]{0,1:T(8,128)}, u32[]{:S(2)}, u32[]{:S(2)}) collective-permute-start(f32[1152,512]{0,1:T(8,128)} %all-reduce.12.cloned.1.call-done), channel_id=1, source_target_pairs={{0,8},{1,24},{2,40},{3,56},{4,72},{5,88},{6,104},{7,120},{8,0},{9,... | collective-permute-start | bytes 7077896 | tf_op jit(solution)/shard_map/ppermute | solution.py:33
  269.6 15.8 %copy-start.23 = (f32[128,256]{1,0:T(8,128)}, f32[128,256]{1,0:T(8,128)S(1)}, u32[]{:S(2)}) copy-start(f32[128,256]{1,0:T(8,128)S(1)} %fusion.46) | copy-start | bytes 393220
  270.2 15.2 %copy-start.27 = (f32[128,256]{1,0:T(8,128)}, f32[128,256]{1,0:T(8,128)S(1)}, u32[]{:S(2)}) copy-start(f32[128,256]{1,0:T(8,128)S(1)} %fusion.61) | copy-start | bytes 393220
  272.9 12.6 copy-start.37
  285.4 4.3 copy-start.4
  285.4 4.3 copy-start.6
  314.2 395.6 %all-reduce.24.cloned.1.call-start = ((), (), s32[]{:S(2)}) async-start(), calls=%async_computation.6 | async-start | bytes 2883584 | tf_op jit(solution)/shard_map/psum | solution.py:97
  318.7 591.9 %all-reduce.16.cloned.1.call-start = ((), (), s32[]{:S(2)}) async-start(), calls=%async_computation.2 | async-start | bytes 524288 | tf_op jit(solution)/shard_map/psum | solution.py:86
  612.2 58.2 %copy-start.41 = (s32[2,2]{1,0:T(2,128)S(1)}, s32[2,2]{1,0:T(2,128)}, u32[]{:S(2)}) copy-start(s32[2,2]{1,0:T(2,128)} %copy-done.40) | copy-start | bytes 52
  698.7 5.8 copy-start.34
  709.8 3.5 copy-start.30
  709.8 9.2 copy-start.15
  709.8 9.2 copy-start.33
  709.8 9.6 copy-start.11
  709.8 9.6 copy-start.22
  713.3 31.4 %collective-permute-start.3 = (f32[1152,256]{0,1:T(8,128)S(1)}, f32[1152,256]{0,1:T(8,128)S(1)}, u32[]{:S(2)}, u32[]{:S(2)}) collective-permute-start(f32[1152,256]{0,1:T(8,128)S(1)} %copy-done.30), channel_id=1, source_target_pairs={{0,0},{1,16},{2,32},{3,48},{4,64},{5,80},{6,96},{7,112},{8,8},{9,2... | collective-permute-start | bytes 3538952 | tf_op jit(solution)/shard_map/ppermute | solution.py:32
  717.5 28.7 %collective-permute-start.2 = (f32[1152,256]{0,1:T(8,128)S(1)}, f32[1152,256]{0,1:T(8,128)S(1)}, u32[]{:S(2)}, u32[]{:S(2)}) collective-permute-start(f32[1152,256]{0,1:T(8,128)S(1)} %copy-done.30), channel_id=1, source_target_pairs={{0,8},{1,24},{2,40},{3,56},{4,72},{5,88},{6,104},{7,120},{8,0},{9,... | collective-permute-start | bytes 3538952 | tf_op jit(solution)/shard_map/ppermute | solution.py:33
  719.4 2.5 copy-start.26
  723.3 23.1 %copy-start.16 = (f32[2304,256]{1,0:T(8,128)S(1)}, f32[2304,256]{1,0:T(8,128)}, u32[]{:S(2)}) copy-start(f32[2304,256]{1,0:T(8,128)} %convolution_multiply_fusion.1) | copy-start | bytes 7077892
  723.3 29.5 %slice-start.3 = ((s8[10616832]{0:T(1024)(128)(4,1)}), s8[4194304]{0:T(1024)(128)(4,1)S(1)}, s32[]{:S(2)}) async-start(s8[10616832]{0:T(1024)(128)(4,1)} %bitcast.192), calls=%async_computation.10 | async-start | bytes 8388608
  725.7 27.0 %slice-start.4 = ((s8[10616832]{0:T(1024)(128)(4,1)}), s8[4194304]{0:T(1024)(128)(4,1)S(1)}, s32[]{:S(2)}) async-start(s8[10616832]{0:T(1024)(128)(4,1)} %bitcast.192), calls=%async_computation.11 | async-start | bytes 8388608
  746.4 6.4 slice-start.5
  752.8 19.4 %copy-start.5 = (f32[1152,512]{0,1:T(8,128)S(1)}, f32[1152,512]{0,1:T(8,128)}, u32[]{:S(2)}) copy-start(f32[1152,512]{0,1:T(8,128)} %copy-done.4) | copy-start | bytes 7077892
  752.8 19.4 %copy-start.7 = (f32[1152,512]{0,1:T(8,128)S(1)}, f32[1152,512]{0,1:T(8,128)}, u32[]{:S(2)}) copy-start(f32[1152,512]{0,1:T(8,128)} %copy-done.6) | copy-start | bytes 7077892
  752.8 19.4 %copy-start.38 = (pred[2304]{0:T(1024)(128)(4,1)S(1)}, pred[2304]{0:T(1024)(128)(4,1)}, u32[]{:S(2)}) copy-start(pred[2304]{0:T(1024)(128)(4,1)} %fusion.69) | copy-start | bytes 6916
  779.0 300.5 %all-reduce.22.cloned.1.call-start = ((), (), s32[]{:S(2)}) async-start(), calls=%async_computation.5 | async-start | bytes 2883584 | tf_op jit(solution)/shard_map/psum | solution.py:86
  912.4 85.5 %copy-start.1 = (f32[2304,256]{0,1:T(8,128)S(1)}, f32[2304,256]{0,1:T(8,128)}, u32[]{:S(2)}) copy-start(f32[2304,256]{0,1:T(8,128)} %copy-done) | copy-start | bytes 7077892
  912.4 85.5 %copy-start.35 = (s32[2304]{0:T(1024)S(1)}, s32[2304]{0:T(1024)}, u32[]{:S(2)}) copy-start(s32[2304]{0:T(1024)} %fusion.68) | copy-start | bytes 27652
  994.8 2.4 copy-start.24
  1016.3 299.0 %all-reduce.18.cloned.1.call-start = ((), (), s32[]{:S(2)}) async-start(), calls=%async_computation.3 | async-start | bytes 524288 | tf_op jit(solution)/shard_map/psum | solution.py:100
  1019.0 4.8 copy-start.8
  1023.8 63.4 %copy-start.25 = (f32[128,256]{1,0:T(8,128)S(1)}, f32[128,256]{1,0:T(8,128)}, u32[]{:S(2)}) copy-start(f32[128,256]{1,0:T(8,128)} %copy-done.24) | copy-start | bytes 393220
  1023.8 63.4 %copy-start.29 = (f32[128,256]{1,0:T(8,128)S(1)}, f32[128,256]{1,0:T(8,128)}, u32[]{:S(2)}) copy-start(f32[128,256]{1,0:T(8,128)} %copy-done.28) | copy-start | bytes 393220
  1079.4 246.6 %collective-permute-start.5 = (f32[1152,256]{0,1:T(8,128)}, f32[1152,256]{0,1:T(8,128)}, u32[]{:S(2)}, u32[]{:S(2)}) collective-permute-start(f32[1152,256]{0,1:T(8,128)} %get-tuple-element.71), channel_id=1, source_target_pairs={{0,0},{1,16},{2,32},{3,48},{4,64},{5,80},{6,96},{7,112},{8,8},{9,2... | collective-permute-start | bytes 3538952 | tf_op jit(solution)/shard_map/ppermute | solution.py:32
  1086.7 239.3 %collective-permute-start.4 = (f32[1152,256]{0,1:T(8,128)}, f32[1152,256]{0,1:T(8,128)}, u32[]{:S(2)}, u32[]{:S(2)}) collective-permute-start(f32[1152,256]{0,1:T(8,128)} %get-tuple-element.71), channel_id=1, source_target_pairs={{0,8},{1,24},{2,40},{3,56},{4,72},{5,88},{6,104},{7,120},{8,0},{9,... | collective-permute-start | bytes 3538952 | tf_op jit(solution)/shard_map/ppermute | solution.py:33
  1088.8 61.4 %copy-start.20 = (f32[256,256]{1,0:T(8,128)S(1)}, f32[256,256]{1,0:T(8,128)}, u32[]{:S(2)}) copy-start(f32[256,256]{1,0:T(8,128)} %copy-done.19) | copy-start | bytes 786436
  1151.6 170.1 %copy-start.9 = (f32[1152,256]{0,1:T(8,128)S(1)}, f32[1152,256]{0,1:T(8,128)}, u32[]{:S(2)}) copy-start(f32[1152,256]{0,1:T(8,128)} %copy-done.8) | copy-start | bytes 3538948
  1152.2 163.1 %copy-start.17 = (f32[256,256]{1,0:T(8,128)}, f32[256,256]{1,0:T(8,128)S(1)}, u32[]{:S(2)}) copy-start(f32[256,256]{1,0:T(8,128)S(1)} %fusion.106) | copy-start | bytes 786436
  1316.7 7.1 copy-start.3
  1318.2 14.0 %slice-start = ((s8[10616832]{0:T(1024)(128)(4,1)}), s8[4194304]{0:T(1024)(128)(4,1)S(1)}, s32[]{:S(2)}) async-start(s8[10616832]{0:T(1024)(128)(4,1)} %bitcast.190), calls=%async_computation.7 | async-start | bytes 8388608
  1323.8 8.4 slice-start.1
  1326.0 2.0 copy-start.18
  1326.0 6.3 slice-start.2
  (15 other events, 15.8 us)
Sparse Core Ops, SparseCore 0:
  13.3 144.8 all-reduce.13
  161.1 62.1 all-reduce.11
  314.3 297.8 all-reduce.19
  615.3 60.7 all-reduce.23
  779.1 131.4 all-reduce.15
  1016.5 62.9 all-reduce.21
  1084.2 231.1 all-reduce.17
where the time goes:
time: 1380 us; the launch traced here: 1370 us
  waiting for transfers between devices  835 us (61%)
  other arithmetic  255 us (18%)
  matrix products  185 us (13%)
  local copies, waits for them, and re-layouts  51.6 us (4%)
  starting transfers between devices  21.4 us (2%)
  between operations  20.9 us (2%)
    psum x2, waiting for transfers between devices, body(): gram0, top0 = lax.psum((g_loc, top_loc), ('row', 'col'))  430 us
    psum x2, waiting for transfers between devices, body(): gram, top = lax.psum((g_part, top_part), 'col')  170 us
    psum x1, waiting for transfers between devices, body(): curv = lax.psum(mm_tn(y_r, xp), ('row', 'col'))  163 us
    dot_general x23, matrix products, mm_nt(): return lax.dot_general(a, b, (((1,), (1,)), ((), ())), precision=HIGH)  108 us
    another operation x14, other arithmetic, small_factors(): second = jnp.linalg.cholesky(mm_nt(shifted, shifted))  76.6 us
    another operation x13, other arithmetic, small_factors(): low = jnp.linalg.cholesky(gram)  75.8 us
    dot_general x9, matrix products, mm(): return jnp.dot(a, b, precision=HIGH)  44.4 us
    another operation x4, other arithmetic, small_factors(): second_inv = jax.scipy.linalg.solve_triangular(second, identity, lower=True)  42.7 us
  transfers between devices with their start and end apart: 13, of which 9 were waited for; matrix products, arithmetic and copies ran while one was open for 20% of the time, Pallas kernels for 0%

commit v1 on v0

--- a/solution.py
+++ b/solution.py
@@ -97,7 +97,7 @@
             x_r, x_e = lax.psum((xp, ext), "col")
         else:
             x_r = lax.psum(xp, "col")
-        curv = lax.psum(mm_tn(y_r, xp), ("row", "col"))
+        curv = lax.psum(lax.psum(mm_tn(y_r, xp), "col"), "row")
         x_c = transpose_exchange(x_r, rows, cols)
         middle = mm_nt(mm(transform, curv), transform)
         w_r = mm_nt(x_r, transform) - 0.5 * mm(y_r, middle)

time: 1380 us -> 1230 us (0.89)
  waiting for transfers between devices: 835 us -> 713 us
    psum x2 -> x3, waiting for transfers between devices: 163 us -> 466 us  [body(): curv = lax.psum(lax.psum(mm_tn(y_r, xp), 'col'), 'row')]
    psum x2 -> x1, waiting for transfers between devices: 430 us -> 142 us  [body(): gram0, top0 = lax.psum((g_loc, top_loc), ('row', 'col'))]
    psum x2, waiting for transfers between devices: 170 us -> 102 us  [body(): gram, top = lax.psum((g_part, top_part), 'col')]
    psum x1, waiting for transfers between devices: 41.3 us -> 2.12 us  [body(): colb = lax.psum(jnp.where(col_zero, a[:, :width], 0.0), 'col')]
    ppermute x3, waiting for transfers between devices: 18.9 us -> 0.01 us  [transpose_exchange(): got1 = lax.ppermute(x, both, first)]
  transfers between devices with their start and end apart: 13 -> 13, of which waited for: 9 -> 7; matrix products, arithmetic and copies ran while one was open for 20% -> 20% of each run, Pallas kernels for 0% -> 0%
where the time goes in v1:
time: 1230 us
  waiting for transfers between devices  713 us (58%)
  other arithmetic  245 us (20%)
  matrix products  182 us (15%)
  local copies, waits for them, and re-layouts  41.1 us (3%)
  starting transfers between devices  23.1 us (2%)
  between operations  21 us (2%)
    psum x3, waiting for transfers between devices, body(): curv = lax.psum(lax.psum(mm_tn(y_r, xp), 'col'), 'row')  466 us
    psum x1, waiting for transfers between devices, body(): gram0, top0 = lax.psum((g_loc, top_loc), ('row', 'col'))  142 us
    dot_general x23, matrix products, mm_nt(): return lax.dot_general(a, b, (((1,), (1,)), ((), ())), precision=HIGH)  109 us
    psum x2, waiting for transfers between devices, body(): gram, top = lax.psum((g_part, top_part), 'col')  102 us
    another operation x13, other arithmetic, small_factors(): low = jnp.linalg.cholesky(gram)  76 us
    another operation x14, other arithmetic, small_factors(): second = jnp.linalg.cholesky(mm_nt(shifted, shifted))  69.2 us
    dot_general x9, matrix products, mm(): return jnp.dot(a, b, precision=HIGH)  43.4 us
    another operation x5, other arithmetic, small_factors(): low_inv = jax.scipy.linalg.solve_triangular(low, identity, lower=True)  42.6 us
  transfers between devices with their start and end apart: 13, of which 7 were waited for; matrix products, arithmetic and copies ran while one was open for 20% of the time, Pallas kernels for 0%

profile of v1, /device:TPU:1, one launch (start us, length us, event | category | flops | bytes accessed | tf_op | source)
XLA Modules:
  0.0 1226.3 jit_solution(12731197977630868926)
XLA Ops:
  19.9 142.4 %all-reduce.20.cloned.1.call-done = (f32[256,256]{0,1:T(8,128)}, f32[256,256]{0,1:T(8,128)}) async-done(((f32[256,256]{0,1:T(8,128)}, f32[256,256]{0,1:T(8,128)}), (f32[256,256]{0,1:T(8,128)}, f32[256,256]{0,1:T(8,128)})) %all-reduce.20.cloned.1.call-update) | async-done | bytes 524304 | tf_op jit(solution)/shard_map/psum | solution.py:68
  164.4 11.7 cholesky.214
  176.2 9.8 custom-call.17
  186.5 11.7 cholesky.231
  200.3 4.1 while.8
  204.4 19.7 %custom-call.18 = f32[2,128,128]{1,2,0:T(8,128)S(1)} custom-call(f32[2,128,128]{2,1,0:T(8,128)S(1)} %get-tuple-element.30), custom_call_target="InvertDiagBlocksLowerTriangular" | custom-call | tf_op jit(solution)/shard_map/jit(_solve_triangular)/triangular_solve | solution.py:43
  229.0 7.2 collective-permute-start.1
  236.4 11.7 cholesky.248
  248.2 9.8 custom-call.19
  258.5 11.7 cholesky.265
  272.9 4.0 while.9
  276.9 20.7 %custom-call.20 = f32[2,128,128]{1,2,0:T(8,128)} custom-call(f32[2,128,128]{2,1,0:T(8,128)S(1)} %get-tuple-element.31), custom_call_target="InvertDiagBlocksLowerTriangular" | custom-call | tf_op jit(solution)/shard_map/jit(_solve_triangular)/triangular_solve | solution.py:46
  300.3 2.8 broadcast_select_fusion.1
  303.2 4.2 convolution_add_fusion.1
  307.4 2.8 fusion.22
  310.3 19.2 %fusion.94 = f32[256,1152]{1,0:T(8,128)S(1)} fusion(f32[2304,256]{1,0:T(8,128)S(1)} %convolution_add_fusion.1, f32[1152,2304]{1,0:T(8,128)S(1)} %bitcast.193), kind=kOutput, calls=%fused_computation.198 | convolution fusion | flops 8153726976 | bytes 14155776 | tf_op jit(solution)/shard_map/dot_general | solution.py:12
  339.0 196.9 %all-reduce.24.cloned.1.call-done = (f32[256,256]{1,0:T(8,128)}, f32[1152,256]{0,1:T(8,128)}, f32[256,256]{1,0:T(8,128)}) async-done(((f32[256,256]{1,0:T(8,128)}, f32[1152,256]{0,1:T(8,128)}, f32[256,256]{1,0:T(8,128)}), (f32[256,256]{1,0:T(8,128)}, f32[1152,256]{0,1:T(8,128)}, f32[256,256]{1,0:T(8,128)})) %all-reduce.24.cloned.1.call-update) | async-done | bytes 1703952 | tf_op jit(solution)/shard_map/psum | solution.py:100
  536.0 7.1 collective-permute-start.3
  543.3 4.4 fusion.100
  548.8 167.1 %all-reduce.14.cloned.1.call-done = f32[256,256]{1,0:T(8,128)} async-done(((f32[256,256]{1,0:T(8,128)}), f32[256,256]{1,0:T(8,128)}) %all-reduce.14.cloned.1.call-update) | async-done | bytes 262160 | tf_op jit(solution)/shard_map/psum | solution.py:100
  729.2 4.2 convolution_subtract_fusion.6
  735.8 19.2 %convolution_subtract_fusion.3 = f32[1152,2304]{1,0:T(8,128)} fusion(f32[1152,2304]{1,0:T(8,128)S(1)} %bitcast.195, f32[1152,256]{0,1:T(8,128)S(1)} %convolution_add_fusion.3, f32[2304,256]{1,0:T(8,128)S(1)} %convolution_subtract_fusion.6), kind=kOutput, calls=%fused_computation.11 | convolution fusion | flops 8156381184 | bytes 24772608 | tf_op jit(solution)/shard_map/dot_general | solution.py:20
  759.0 2.8 fusion.103
  761.9 14.0 %convolution_subtract_fusion.2 = f32[1152,2304]{1,0:T(8,128)} fusion(f32[1152,2304]{1,0:T(8,128)} %convolution_subtract_fusion.3, f32[1152,256]{1,0:T(8,128)} %copy-done.12, f32[2304,256]{1,0:T(8,128)S(1)} %convolution_add_fusion.1), kind=kOutput, calls=%fused_computation.10 | convolution fusion | flops 8156381184 | bytes 24772608 | tf_op jit(solution)/shard_map/dot_general | solution.py:20
  777.5 42.6 %all-reduce.16.cloned.1.call-done = f32[256,256]{0,1:T(8,128)} async-done(((f32[256,256]{0,1:T(8,128)}), f32[256,256]{0,1:T(8,128)}) %all-reduce.16.cloned.1.call-update) | async-done | bytes 262160 | tf_op jit(solution)/shard_map/psum | solution.py:86
  824.5 13.2 %cholesky.282 = f32[128,128]{1,0:T(8,128)} custom-call(f32[128,128]{1,0:T(8,128)} %cholesky.352), custom_call_target="Cholesky" | custom-call | tf_op jit(solution)/shard_map/jit(cholesky)/cholesky | solution.py:42
  839.9 11.3 custom-call.21
  856.2 13.2 %cholesky.299 = f32[128,128]{1,0:T(8,128)} custom-call(f32[128,128]{1,0:T(8,128)} %convolution_subtract_fusion.14), custom_call_target="Cholesky" | custom-call | tf_op jit(solution)/shard_map/jit(cholesky)/cholesky | solution.py:42
  875.3 6.9 while.10
  875.9 2.9 bitcast_dynamic-update-slice_fusion.10
  879.4 2.8 bitcast_dynamic-update-slice_fusion.10
  882.2 21.3 %custom-call.22 = f32[2,128,128]{1,2,0:T(8,128)} custom-call(f32[2,128,128]{2,1,0:T(8,128)} %get-tuple-element.32), custom_call_target="InvertDiagBlocksLowerTriangular" | custom-call | tf_op jit(solution)/shard_map/jit(_solve_triangular)/triangular_solve | solution.py:43
  907.8 4.4 convolution_add_fusion
  913.6 11.2 fusion.104
  932.3 3.1 copy.15
  935.4 59.4 %all-reduce.22.cloned.1.call-done = (f32[256,256]{0,1:T(8,128)}, f32[256,256]{1,0:T(8,128)}, f32[1152,256]{0,1:T(8,128)}) async-done(((f32[256,256]{0,1:T(8,128)}, f32[256,256]{1,0:T(8,128)}, f32[1152,256]{0,1:T(8,128)}), (f32[256,256]{0,1:T(8,128)}, f32[256,256]{1,0:T(8,128)}, f32[1152,256]{0,1:T(8,128)})) %all-reduce.22.cloned.1.call-update) | async-done | bytes 1703952 | tf_op jit(solution)/shard_map/psum | solution.py:86
  994.8 7.2 collective-permute-start.5
  1004.7 11.7 cholesky.316
  1017.1 9.8 custom-call.23
  1027.5 11.7 cholesky.333
  1041.1 3.9 while.11
  1045.1 19.8 %custom-call.24 = f32[2,128,128]{1,2,0:T(8,128)S(1)} custom-call(f32[2,128,128]{2,1,0:T(8,128)S(1)} %get-tuple-element.33), custom_call_target="InvertDiagBlocksLowerTriangular" | custom-call | tf_op jit(solution)/shard_map/jit(_solve_triangular)/triangular_solve | solution.py:46
  1067.7 4.5 fusion.110
  1072.3 102.4 %all-reduce.18.cloned.1.call-done = f32[256,256]{1,0:T(8,128)} async-done(((f32[256,256]{1,0:T(8,128)}), f32[256,256]{1,0:T(8,128)}) %all-reduce.18.cloned.1.call-update) | async-done | bytes 262160 | tf_op jit(solution)/shard_map/psum | solution.py:100
  1177.7 3.3 fusion.2
  1185.1 4.3 convolution_subtract_fusion.4
  1189.4 18.1 %convolution_subtract_fusion.1 = f32[1152,2304]{1,0:T(8,128)S(1)} fusion(f32[1152,2304]{1,0:T(8,128)S(1)} %bitcast.191, f32[1152,256]{0,1:T(8,128)S(1)} %copy-done.9, f32[2304,256]{1,0:T(8,128)S(1)} %convolution_subtract_fusion.4), kind=kOutput, calls=%fused_computation.9 | convolution fusion | flops 8156381184 | bytes 24772608 | tf_op jit(solution)/shard_map/dot_general | solution.py:20
  1207.5 11.5 convolution_subtract_fusion
  (259 shorter events, 114.1 us)
Async XLA Ops:
  7.2 155.1 %all-reduce.20.cloned.1.call-start = ((), (), s32[]{:S(2)}) async-start(), calls=%async_computation.4 | async-start | bytes 1048576 | tf_op jit(solution)/shard_map/psum | solution.py:68
  11.7 217.4 %all-reduce.12.cloned.1.call-start = ((), (), s32[]{:S(2)}) async-start(), calls=%async_computation | async-start | bytes 4718592 | tf_op jit(solution)/shard_map/psum | solution.py:62
  16.8 519.1 %all-reduce.24.cloned.1.call-start = ((), (), s32[]{:S(2)}) async-start(), calls=%async_computation.6 | async-start | bytes 3407872 | tf_op jit(solution)/shard_map/psum | solution.py:100
  19.9 204.8 %copy-start.18 = (f32[256,256]{1,0:T(8,128)}, f32[256,256]{1,0:T(8,128)S(1)}, u32[]{:S(2)}) copy-start(f32[256,256]{1,0:T(8,128)S(1)} %fusion.39) | copy-start | bytes 786436
  163.4 61.7 %copy-start.33 = (f32[256,256]{0,1:T(8,128)S(1)}, f32[256,256]{0,1:T(8,128)}, u32[]{:S(2)}) copy-start(f32[256,256]{0,1:T(8,128)} %get-tuple-element.69) | copy-start | bytes 786436
  224.4 73.2 %copy-start.21 = (f32[128,256]{1,0:T(8,128)}, f32[128,256]{1,0:T(8,128)S(1)}, u32[]{:S(2)}) copy-start(f32[128,256]{1,0:T(8,128)S(1)} %fusion.46) | copy-start | bytes 393220
  225.0 72.6 %copy-start.26 = (f32[128,256]{1,0:T(8,128)}, f32[128,256]{1,0:T(8,128)S(1)}, u32[]{:S(2)}) copy-start(f32[128,256]{1,0:T(8,128)S(1)} %fusion.61) | copy-start | bytes 393220
  229.0 71.2 %collective-permute-start.1 = (f32[1152,512]{0,1:T(8,128)}, f32[1152,512]{0,1:T(8,128)}, u32[]{:S(2)}, u32[]{:S(2)}) collective-permute-start(f32[1152,512]{0,1:T(8,128)} %all-reduce.12.cloned.1.call-done), channel_id=1, source_target_pairs={{0,0},{1,16},{2,32},{3,48},{4,64},{5,80},{6,96},{7,112},{8,8},{9,2... | collective-permute-start | bytes 7077896 | tf_op jit(solution)/shard_map/ppermute | solution.py:32
  236.2 64.0 %collective-permute-start = (f32[1152,512]{0,1:T(8,128)}, f32[1152,512]{0,1:T(8,128)}, u32[]{:S(2)}, u32[]{:S(2)}) collective-permute-start(f32[1152,512]{0,1:T(8,128)} %all-reduce.12.cloned.1.call-done), channel_id=1, source_target_pairs={{0,8},{1,24},{2,40},{3,56},{4,72},{5,88},{6,104},{7,120},{8,0},{9,... | collective-permute-start | bytes 7077896 | tf_op jit(solution)/shard_map/ppermute | solution.py:33
  276.9 26.3 %copy-start.30 = (f32[256,256]{1,0:T(8,128)}, f32[256,256]{1,0:T(8,128)S(1)}, u32[]{:S(2)}) copy-start(f32[256,256]{1,0:T(8,128)S(1)} %get-tuple-element.327) | copy-start | bytes 786436
  276.9 26.3 %copy-start.40 = (s32[2,2]{1,0:T(2,128)}, s32[2,2]{1,0:T(2,128)S(1)}, u32[]{:S(2)}) copy-start(s32[2,2]{1,0:T(2,128)S(1)} %get-tuple-element.363) | copy-start | bytes 52
  300.2 3.0 copy-start.22
  300.2 3.0 copy-start.27
  300.3 10.0 slice-start.3
  300.3 10.0 slice-start.4
  303.2 4.3 copy-start.4
  303.2 4.3 copy-start.6
  303.2 7.1 slice-start.5
  332.5 383.4 %all-reduce.14.cloned.1.call-start = ((), (), s32[]{:S(2)}) async-start(), calls=%async_computation.1 | async-start | bytes 524288 | tf_op jit(solution)/shard_map/psum | solution.py:100
  536.0 191.3 %collective-permute-start.3 = (f32[1152,256]{0,1:T(8,128)}, f32[1152,256]{0,1:T(8,128)}, u32[]{:S(2)}, u32[]{:S(2)}) collective-permute-start(f32[1152,256]{0,1:T(8,128)} %get-tuple-element.74), channel_id=1, source_target_pairs={{0,0},{1,16},{2,32},{3,48},{4,64},{5,80},{6,96},{7,112},{8,8},{9,2... | collective-permute-start | bytes 3538952 | tf_op jit(solution)/shard_map/ppermute | solution.py:32
  543.1 184.2 %collective-permute-start.2 = (f32[1152,256]{0,1:T(8,128)}, f32[1152,256]{0,1:T(8,128)}, u32[]{:S(2)}, u32[]{:S(2)}) collective-permute-start(f32[1152,256]{0,1:T(8,128)} %get-tuple-element.74), channel_id=1, source_target_pairs={{0,8},{1,24},{2,40},{3,56},{4,72},{5,88},{6,104},{7,120},{8,0},{9,... | collective-permute-start | bytes 3538952 | tf_op jit(solution)/shard_map/ppermute | solution.py:33
  543.2 276.9 %all-reduce.16.cloned.1.call-start = ((), (), s32[]{:S(2)}) async-start(), calls=%async_computation.2 | async-start | bytes 524288 | tf_op jit(solution)/shard_map/psum | solution.py:86
  543.3 4.4 copy-start.14
  543.3 4.4 copy-start.34
  717.4 3.5 copy-start.11
  717.4 3.5 copy-start.31
  725.1 10.7 slice-start.6
  727.2 8.5 slice-start.7
  729.2 6.6 slice-start.8
  735.8 19.2 %copy-start.5 = (f32[1152,512]{0,1:T(8,128)S(1)}, f32[1152,512]{0,1:T(8,128)}, u32[]{:S(2)}) copy-start(f32[1152,512]{0,1:T(8,128)} %copy-done.4) | copy-start | bytes 7077892
  735.8 19.2 %copy-start.7 = (f32[1152,512]{0,1:T(8,128)S(1)}, f32[1152,512]{0,1:T(8,128)}, u32[]{:S(2)}) copy-start(f32[1152,512]{0,1:T(8,128)} %copy-done.6) | copy-start | bytes 7077892
  735.8 19.2 %copy-start.38 = (pred[2304]{0:T(1024)(128)(4,1)S(1)}, pred[2304]{0:T(1024)(128)(4,1)}, u32[]{:S(2)}) copy-start(pred[2304]{0:T(1024)(128)(4,1)} %get-tuple-element.120) | copy-start | bytes 6916
  761.8 232.9 %all-reduce.22.cloned.1.call-start = ((), (), s32[]{:S(2)}) async-start(), calls=%async_computation.5 | async-start | bytes 3407872 | tf_op jit(solution)/shard_map/psum | solution.py:86
  775.9 99.4 %copy-start.41 = (s32[2,2]{1,0:T(2,128)S(1)}, s32[2,2]{1,0:T(2,128)}, u32[]{:S(2)}) copy-start(s32[2,2]{1,0:T(2,128)} %copy-done.40) | copy-start | bytes 52
  822.0 85.8 %copy-start.1 = (f32[2304,256]{0,1:T(8,128)S(1)}, f32[2304,256]{0,1:T(8,128)}, u32[]{:S(2)}) copy-start(f32[2304,256]{0,1:T(8,128)} %copy-done) | copy-start | bytes 7077892
  822.0 85.8 %copy-start.35 = (s32[2304]{0:T(1024)S(1)}, s32[2304]{0:T(1024)}, u32[]{:S(2)}) copy-start(s32[2304]{0:T(1024)} %get-tuple-element.118) | copy-start | bytes 27652
  928.8 3.5 copy-start.8
  930.7 244.0 %all-reduce.18.cloned.1.call-start = ((), (), s32[]{:S(2)}) async-start(), calls=%async_computation.3 | async-start | bytes 524288 | tf_op jit(solution)/shard_map/psum | solution.py:100
  932.3 70.1 %copy-start.24 = (f32[128,256]{1,0:T(8,128)S(1)}, f32[128,256]{1,0:T(8,128)}, u32[]{:S(2)}) copy-start(f32[128,256]{1,0:T(8,128)} %copy-done.23) | copy-start | bytes 393220
  932.3 70.2 %copy-start.29 = (f32[128,256]{1,0:T(8,128)S(1)}, f32[128,256]{1,0:T(8,128)}, u32[]{:S(2)}) copy-start(f32[128,256]{1,0:T(8,128)} %copy-done.28) | copy-start | bytes 393220
  994.8 188.4 %collective-permute-start.5 = (f32[1152,256]{0,1:T(8,128)}, f32[1152,256]{0,1:T(8,128)}, u32[]{:S(2)}, u32[]{:S(2)}) collective-permute-start(f32[1152,256]{0,1:T(8,128)} %get-tuple-element.72), channel_id=1, source_target_pairs={{0,0},{1,16},{2,32},{3,48},{4,64},{5,80},{6,96},{7,112},{8,8},{9,2... | collective-permute-start | bytes 3538952 | tf_op jit(solution)/shard_map/ppermute | solution.py:32
  1002.0 181.2 %collective-permute-start.4 = (f32[1152,256]{0,1:T(8,128)}, f32[1152,256]{0,1:T(8,128)}, u32[]{:S(2)}, u32[]{:S(2)}) collective-permute-start(f32[1152,256]{0,1:T(8,128)} %get-tuple-element.72), channel_id=1, source_target_pairs={{0,8},{1,24},{2,40},{3,56},{4,72},{5,88},{6,104},{7,120},{8,0},{9,... | collective-permute-start | bytes 3538952 | tf_op jit(solution)/shard_map/ppermute | solution.py:33
  1004.1 60.8 %copy-start.19 = (f32[256,256]{1,0:T(8,128)S(1)}, f32[256,256]{1,0:T(8,128)}, u32[]{:S(2)}) copy-start(f32[256,256]{1,0:T(8,128)} %copy-done.18) | copy-start | bytes 786436
  1066.4 111.2 %copy-start.9 = (f32[1152,256]{0,1:T(8,128)S(1)}, f32[1152,256]{0,1:T(8,128)}, u32[]{:S(2)}) copy-start(f32[1152,256]{0,1:T(8,128)} %copy-done.8) | copy-start | bytes 3538948
  1067.7 113.3 %copy-start.3 = (f32[2304,256]{1,0:T(8,128)S(1)}, f32[2304,256]{1,0:T(8,128)}, u32[]{:S(2)}) copy-start(f32[2304,256]{1,0:T(8,128)} %copy-done.2) | copy-start | bytes 7077892
  1174.7 14.7 %slice-start = ((s8[10616832]{0:T(1024)(128)(4,1)}), s8[4194304]{0:T(1024)(128)(4,1)S(1)}, s32[]{:S(2)}) async-start(s8[10616832]{0:T(1024)(128)(4,1)} %bitcast.190), calls=%async_computation.7 | async-start | bytes 8388608
  1181.0 8.4 slice-start.1
  1183.1 6.3 slice-start.2
  (18 other events, 29.4 us)
Sparse Core Ops, SparseCore 0:
  13.5 148.7 all-reduce.19
  165.4 63.6 all-reduce.11
  332.6 203.3 all-reduce.23
  543.3 172.5 all-reduce.13
  761.9 58.1 all-reduce.15
  930.9 63.8 all-reduce.21
  1004.2 170.4 all-reduce.17
